TPU v7x, 32 devices: a whole 2x2x4 slice. The times are simulated.
32 devices in a mesh: pts: 2 (over core), cen: 16 (over z, y, x).
Axes of the slice: x: 2, y: 2, z: 4, core: 2. Of those that a mesh axis runs over, the one named last changes fastest.
Arguments:
- points: bfloat16 [2, 1024, 256], P(None, ('pts', 'cen')), may hold values from -4096 to 4096, as said below
- centroids: float32 [16384, 256], P('cen'), may hold values from -6 to 6, as said below
Outputs:
- new_centroids: float32 [16384, 256], P('cen')
- energy: float32 [2, 1024], P(None, 'pts')
Inputs may be any that keep to these rules, and one draw needn't show every extreme that they name: Real-valued points. Real-valued centroids.
All inputs are finite; a program needn't handle non-finite values.
Results may differ from a plain program's by a relative error of at most 0.0003.
The roundings to bfloat16 on the way count: a program that leaves them out, or rounds other values in their place, can miss the bound.
Values may be sent and summed in bfloat16 or wider, within the bound.
A program may use at most 64 MiB of HBM per device.

v0:
```python
import jax
import jax.numpy as jnp
from jax import lax
from jax.sharding import PartitionSpec as P

STEPS = 2
TEMPER = 32.0


def joined(value, axis, join):
    pieces = jax.tree.map(lambda part: lax.all_gather(part, axis), value)
    head = jax.tree.map(lambda part: part[0], pieces)
    tail = jax.tree.map(lambda part: part[1:], pieces)
    running, _ = lax.scan(lambda running, section: (join(running, section), None), head, tail)
    return running


def combine_softmax(first, second):
    top = jnp.maximum(first[0], second[0])
    total = first[1] * jnp.exp(first[0] - top) + second[1] * jnp.exp(second[0] - top)
    return (top, total)


def on_device(points, centroids):
    current = centroids
    energies = []
    for iteration in range(STEPS):
        cent_low = current.astype(jnp.bfloat16)
        cent_sq = jnp.sum(current * current, axis=1)
        segment = lax.all_gather(points[iteration], "cen", axis=0, tiled=True)
        inner = lax.dot_general(
            segment, cent_low, (((1,), (1,)), ((), ())), preferred_element_type=jnp.float32
        )
        logits = (2.0 * inner - cent_sq[None, :]) / TEMPER
        local_top = jnp.max(logits, axis=1)
        local_weights = jnp.exp(logits - local_top[:, None])
        local_total = jnp.sum(local_weights, axis=1)
        top, total = joined((local_top, local_total), "cen", combine_softmax)
        weights = local_weights * jnp.exp(local_top - top)[:, None]
        resp = weights / total[:, None]
        counts = jnp.sum(resp, axis=0)
        sums = lax.dot_general(
            resp.astype(jnp.bfloat16),
            segment,
            (((0,), (0,)), ((), ())),
            preferred_element_type=jnp.float32,
        )
        sums, counts = lax.psum((sums, counts), "pts")
        current = (current + sums) / (1.0 + counts)[:, None]
        energies.append(top + jnp.log(total))
    return (current, jnp.stack(energies))


def solution(mesh):
    placed = (P(None, ("pts", "cen"), None), P("cen", None))
    return jax.shard_map(
        on_device,
        mesh=mesh,
        in_specs=placed,
        out_specs=(P("cen", None), P(None, "pts")),
        check_vma=False,
    )
```

profile of v0, /device:TPU:0, one launch (start us, length us, event | category | flops | bytes accessed | tf_op | source)
XLA Modules:
  0.0 274.8 jit_solution(6816638734251444056)
XLA Ops:
  7.2 1.5 multiply_reduce_fusion.1
  8.7 0.7 fusion.14
  9.5 43.8 %all-gather = bf16[1,512,256]{2,1,0:T(8,128)(2,1)S(1)} all-gather(bf16[1,32,256]{2,1,0:T(8,128)(2,1)S(1)} %get-tuple-element.95), channel_id=2, replica_groups=mesh['pts'=2,'cen'=16] {'cen'}, dimensions={1}, use_global_device_ids=true | all-gather | bytes 278528 | tf_op jit(solution)/shard_map/all_gather | solution.py:30
  53.3 0.6 fusion.15
  53.8 0.5 fusion
  54.3 35.6 %all-gather.7 = f32[16,1,512]{2,1,0:T(1,128)S(1)} all-gather(f32[1,1,512]{2,1,0:T(1,128)S(1)} %bitcast.65), channel_id=4, replica_groups=mesh['pts'=2,'cen'=16] {'cen'}, dimensions={0}, use_global_device_ids=true | all-gather | bytes 34816 | tf_op jit(solution)/shard_map/all_gather | solution.py:11
  89.9 37.6 %all-gather.6 = f32[16,1,512]{2,1,0:T(1,128)S(1)} all-gather(f32[1,1,512]{2,1,0:T(1,128)S(1)} %bitcast.62), channel_id=3, replica_groups=mesh['pts'=2,'cen'=16] {'cen'}, dimensions={0}, use_global_device_ids=true | all-gather | bytes 34816 | tf_op jit(solution)/shard_map/all_gather | solution.py:11
  127.6 0.8 while.24
  128.4 0.6 fusion.13
  129.0 1.5 fusion.4
  130.5 2.5 psum.29
  133.0 36.8 %all-gather.3 = bf16[1,512,256]{2,1,0:T(8,128)(2,1)S(1)} all-gather(bf16[1,32,256]{2,1,0:T(8,128)(2,1)S(1)} %get-tuple-element.94), channel_id=5, replica_groups=mesh['pts'=2,'cen'=16] {'cen'}, dimensions={1}, use_global_device_ids=true | all-gather | bytes 278528 | tf_op jit(solution)/shard_map/all_gather | solution.py:30
  169.8 1.6 multiply_reduce_fusion
  171.4 0.5 fusion.16
  171.9 0.4 fusion.1
  172.4 37.7 %all-gather.9 = f32[16,1,512]{2,1,0:T(1,128)S(1)} all-gather(f32[1,1,512]{2,1,0:T(1,128)S(1)} %bitcast.66), channel_id=7, replica_groups=mesh['pts'=2,'cen'=16] {'cen'}, dimensions={0}, use_global_device_ids=true | all-gather | bytes 34816 | tf_op jit(solution)/shard_map/all_gather | solution.py:11
  210.1 35.6 %all-gather.8 = f32[16,1,512]{2,1,0:T(1,128)S(1)} all-gather(f32[1,1,512]{2,1,0:T(1,128)S(1)} %bitcast.61), channel_id=6, replica_groups=mesh['pts'=2,'cen'=16] {'cen'}, dimensions={0}, use_global_device_ids=true | all-gather | bytes 34816 | tf_op jit(solution)/shard_map/all_gather | solution.py:11
  245.7 0.8 while.25
  246.6 1.6 fusion.2
  248.2 0.5 fusion.8
  248.7 2.5 psum.31
  251.2 0.6 pad_maximum_fusion
  251.8 13.8 %all-reduce.5.cloned.1.call-done = f32[1024,256]{1,0:T(8,128)} async-done(((f32[1024,256]{1,0:T(8,128)}), f32[1024,256]{1,0:T(8,128)}) %all-reduce.5.cloned.1.call-update) | async-done | bytes 1048592 | tf_op jit(solution)/shard_map/psum | solution.py:48
  265.6 2.4 add_divide_fusion
  (87 shorter events, 1.3 us)
Async XLA Ops:
  7.2 46.1 %copy-start = (f32[1024,256]{1,0:T(8,128)S(1)}, f32[1024,256]{1,0:T(8,128)}, u32[]{:S(2)}) copy-start(f32[1024,256]{1,0:T(8,128)} %param.7) | copy-start | bytes 3145732
  7.2 162.7 %all-reduce.3.cloned.1.call-start = ((), (), s32[]{:S(2)}) async-start(), calls=%async_computation | async-start | bytes 2097152 | tf_op jit(solution)/shard_map/psum | solution.py:48
  130.4 135.1 %all-reduce.5.cloned.1.call-start = ((), (), s32[]{:S(2)}) async-start(), calls=%async_computation.1 | async-start | bytes 2097152 | tf_op jit(solution)/shard_map/psum | solution.py:48
  171.4 1.0 copy-start.1
  248.2 17.4 %copy-start.2 = (f32[1024,256]{1,0:T(8,128)S(1)}, f32[1024,256]{1,0:T(8,128)}, u32[]{:S(2)}) copy-start(f32[1024,256]{1,0:T(8,128)} %copy-done.1) | copy-start | bytes 3145732
Sparse Core Ops, SparseCore 0:
  130.6 15.2 all-reduce.2
  248.3 17.1 all-reduce.4
where the time goes:
time: 275 us
  blocking collectives  232 us (84%)
  between operations  14.1 us (5%)
  waiting for transfers between devices  13.8 us (5%)
  other arithmetic  8.64 us (3%)
  matrix products  4.11 us (1%)
    all_gather x4, blocking collectives, joined(): pieces = jax.tree.map(lambda part: lax.all_gather(part, axis), value)  147 us
    all_gather x2, blocking collectives, on_device(): segment = lax.all_gather(points[iteration], 'cen', axis=0, tiled=True)  80.6 us
    psum x2, waiting for transfers between devices, on_device(): sums, counts = lax.psum((sums, counts), 'pts')  13.8 us
  transfers between devices with their start and end apart: 2, of which 1 were waited for; matrix products, arithmetic and copies ran while one was open for 0% of the time, Pallas kernels for 0%

commit v1 on v0

--- a/solution.py
+++ b/solution.py
@@ -5,6 +5,27 @@
 
 STEPS = 2
 TEMPER = 32.0
+
+
+def in_order(pieces, dim):
+    pieces = jnp.moveaxis(pieces, 0, dim)
+    shape = pieces.shape
+    return pieces.reshape(*shape[:dim], shape[dim] * shape[dim + 1], *shape[dim + 2 :])
+
+
+def doubled(x, axis):
+    peers, index = (lax.axis_size(axis), lax.axis_index(axis))
+    tiles, bit = (x[None], 1)
+    while bit < peers:
+        received = lax.ppermute(tiles, axis, [(i, i ^ bit) for i in range(peers)])
+        low = index & bit == 0
+        tiles = jnp.concatenate([jnp.where(low, tiles, received), jnp.where(low, received, tiles)])
+        bit *= 2
+    return tiles
+
+
+def doubled_up(x, axis, dim):
+    return in_order(doubled(x, axis), dim)
 
 
 def joined(value, axis, join):
@@ -27,7 +48,7 @@
     for iteration in range(STEPS):
         cent_low = current.astype(jnp.bfloat16)
         cent_sq = jnp.sum(current * current, axis=1)
-        segment = lax.all_gather(points[iteration], "cen", axis=0, tiled=True)
+        segment = doubled_up(points[iteration], "cen", 0)
         inner = lax.dot_general(
             segment, cent_low, (((1,), (1,)), ((), ())), preferred_element_type=jnp.float32
         )

time: 275 us -> 257 us (0.935); the launches traced: 275 us -> 254 us
  blocking collectives: 232 us -> 158 us
  waiting for transfers between devices: 13.8 us -> 36.8 us
  starting transfers between devices: 0.08 us -> 15.2 us
  local copies, waits for them, and re-layouts: 1.24 us -> 13.4 us
    all_gather x2 -> x0, blocking collectives: 80.6 us -> none  [on_device(): segment = lax.all_gather(points[iteration], 'cen', axis=0, tiled=True)]
    ppermute x0 -> x8, starting transfers between devices: none -> 15.1 us  [doubled(): received = lax.ppermute(tiles, axis, [(i, i ^ bit) for i in range(peers)])]
    ppermute x0 -> x8, waiting for transfers between devices: none -> 14.6 us  [doubled(): received = lax.ppermute(tiles, axis, [(i, i ^ bit) for i in range(peers)])]
    dynamic_slice x30, local copies, waits for them, and re-layouts: 0.35 us -> 11.4 us  [joined(): lax.scan(lambda running, section: (join(running, section), None), head, t...]
    psum x2, waiting for transfers between devices: 13.8 us -> 22.1 us  [on_device(): sums, counts = lax.psum((sums, counts), 'pts')]
    all_gather x4, blocking collectives: 147 us -> 153 us  [joined(): pieces = jax.tree.map(lambda part: lax.all_gather(part, axis), value)]
  transfers between devices with their start and end apart: 2 -> 10, of which waited for: 1 -> 8; matrix products, arithmetic and copies ran while one was open for 0% -> 7% of each run, Pallas kernels for 0% -> 0%
where the time goes in v1:
time: 257 us; the launch traced here: 254 us
  blocking collectives  158 us (61%)
  waiting for transfers between devices  36.8 us (14%)
  starting transfers between devices  15.2 us (6%)
  between operations  14.2 us (6%)
  local copies, waits for them, and re-layouts  13.4 us (5%)
  other arithmetic  11.3 us (4%)
  matrix products  4.08 us (2%)
    all_gather x4, blocking collectives, joined(): pieces = jax.tree.map(lambda part: lax.all_gather(part, axis), value)  153 us
    psum x2, waiting for transfers between devices, on_device(): sums, counts = lax.psum((sums, counts), 'pts')  22.1 us
    ppermute x8, starting transfers between devices, doubled(): received = lax.ppermute(tiles, axis, [(i, i ^ bit) for i in range(peers)])  15.1 us
    ppermute x8, waiting for transfers between devices, doubled(): received = lax.ppermute(tiles, axis, [(i, i ^ bit) for i in range(peers)])  14.6 us
    dynamic_slice x30, local copies, waits for them, and re-layouts, joined(): lax.scan(lambda running, section: (join(running, section), None), head, t...  11.4 us
  transfers between devices with their start and end apart: 10, of which 8 were waited for; matrix products, arithmetic and copies ran while one was open for 7% of the time, Pallas kernels for 0%

profile of v1, /device:TPU:0, one launch (start us, length us, event | category | flops | bytes accessed | tf_op | source)
XLA Modules:
  0.0 253.9 jit_solution(6781056100567142953)
XLA Ops:
  8.0 3.0 %collective-permute-start.4 = (bf16[1,32,256]{2,1,0:T(8,128)(2,1)S(1)}, bf16[1,32,256]{2,1,0:T(8,128)(2,1)S(1)}, u32[]{:S(2)}, u32[]{:S(2)}) collective-permute-start(bf16[1,32,256]{2,1,0:T(8,128)(2,1)S(1)} %slice.35), channel_id=1, source_target_pairs={{0,1},{1,0},{2,3},{3,2},{4,5},{5,4},{6,7},{7,6},{8,9},{9,8},{10,11... | collective-permute-start | bytes 49160 | tf_op jit(solution)/shard_map/ppermute | solution.py:20
  11.0 1.7 collective-permute-done.4
  13.4 2.0 collective-permute-start
  15.5 1.7 collective-permute-done
  17.9 2.1 collective-permute-start.1
  22.0 2.1 collective-permute-start.2
  24.1 1.5 collective-permute-start.5
  25.6 1.9 collective-permute-done.2
  27.5 2.6 %collective-permute-start.3 = (bf16[8,32,256]{2,1,0:T(8,128)(2,1)S(1)}, bf16[8,32,256]{2,1,0:T(8,128)(2,1)S(1)}, u32[]{:S(2)}, u32[]{:S(2)}) collective-permute-start(bf16[8,32,256]{2,1,0:T(8,128)(2,1)S(1)} %pad_maximum_fusion.2), channel_id=1, source_target_pairs={{0,8},{1,9},{2,10},{3,11},{4,12},{5,13},{6,14},{7,15},{8,0},{9,1},... | collective-permute-start | bytes 393224 | tf_op jit(solution)/shard_map/ppermute | solution.py:20
  30.2 1.6 collective-permute-start.6
  31.9 3.0 %collective-permute-done.3 = bf16[8,32,256]{2,1,0:T(8,128)(2,1)S(1)} collective-permute-done((bf16[8,32,256]{2,1,0:T(8,128)(2,1)S(1)}, bf16[8,32,256]{2,1,0:T(8,128)(2,1)S(1)}, u32[]{:S(2)}, u32[]{:S(2)}) %collective-permute-start.3) | collective-permute-done | bytes 131104 | tf_op jit(solution)/shard_map/ppermute | solution.py:20
  36.0 41.0 %all-gather.5 = f32[16,1,512]{2,1,0:T(1,128)S(1)} all-gather(f32[1,1,512]{2,1,0:T(1,128)S(1)} %bitcast.62), channel_id=3, replica_groups=mesh['pts'=2,'cen'=16] {'cen'}, dimensions={0}, use_global_device_ids=true | all-gather | bytes 34816 | tf_op jit(solution)/shard_map/all_gather | solution.py:32
  77.0 35.8 %all-gather.4 = f32[16,1,512]{2,1,0:T(1,128)S(1)} all-gather(f32[1,1,512]{2,1,0:T(1,128)S(1)} %bitcast.59), channel_id=2, replica_groups=mesh['pts'=2,'cen'=16] {'cen'}, dimensions={0}, use_global_device_ids=true | all-gather | bytes 34816 | tf_op jit(solution)/shard_map/all_gather | solution.py:32
  114.0 11.6 %while.24 = (s32[]{:T(128)}, f32[512]{0:T(512)S(1)}, f32[512]{0:T(512)S(1)}, f32[15,512]{1,0:T(8,128)}, f32[15,512]{1,0:T(8,128)}, /*index=5*/s32[]{:T(128)}) while((s32[]{:T(128)}, f32[512]{0:T(512)S(1)}, f32[512]{0:T(512)S(1)}, f32[15,512]{1,0:T(8,128)}, f32[15,512]{1,0:T(8,128)}, /*index=5*/s32[]{:T(128)}) %tuple.82), condition=%wide.region_4.5_spmd, body=%wide.region_3.4_spmd.sunk | while | flops 3074 | bytes 20553 | solution.py:35
  128.7 5.9 %collective-permute-done.7 = bf16[8,32,256]{2,1,0:T(8,128)(2,1)S(1)} collective-permute-done((bf16[8,32,256]{2,1,0:T(8,128)(2,1)S(1)}, bf16[8,32,256]{2,1,0:T(8,128)(2,1)S(1)}, u32[]{:S(2)}, u32[]{:S(2)}) %collective-permute-start.7) | collective-permute-done | bytes 131104 | tf_op jit(solution)/shard_map/ppermute | solution.py:20
  134.6 2.5 psum.29
  137.1 7.9 %all-reduce.3.cloned.1.call-done = f32[1024,256]{1,0:T(8,128)} async-done(((f32[1024,256]{1,0:T(8,128)}), f32[1024,256]{1,0:T(8,128)}) %all-reduce.3.cloned.1.call-update) | async-done | bytes 1048592 | tf_op jit(solution)/shard_map/psum | solution.py:69
  145.0 1.6 multiply_reduce_fusion
  147.7 41.0 %all-gather.7 = f32[16,1,512]{2,1,0:T(1,128)S(1)} all-gather(f32[1,1,512]{2,1,0:T(1,128)S(1)} %bitcast.63), channel_id=5, replica_groups=mesh['pts'=2,'cen'=16] {'cen'}, dimensions={0}, use_global_device_ids=true | all-gather | bytes 34816 | tf_op jit(solution)/shard_map/all_gather | solution.py:32
  188.7 35.6 %all-gather.6 = f32[16,1,512]{2,1,0:T(1,128)S(1)} all-gather(f32[1,1,512]{2,1,0:T(1,128)S(1)} %bitcast.58), channel_id=4, replica_groups=mesh['pts'=2,'cen'=16] {'cen'}, dimensions={0}, use_global_device_ids=true | all-gather | bytes 34816 | tf_op jit(solution)/shard_map/all_gather | solution.py:32
  225.7 1.5 fusion.2
  227.3 2.5 psum.31
  230.3 14.3 %all-reduce.5.cloned.1.call-done = f32[1024,256]{1,0:T(8,128)} async-done(((f32[1024,256]{1,0:T(8,128)}), f32[1024,256]{1,0:T(8,128)}) %all-reduce.5.cloned.1.call-update) | async-done | bytes 1048592 | tf_op jit(solution)/shard_map/psum | solution.py:69
  244.6 2.4 add_divide_fusion
  (117 shorter events, 24.7 us)
Async XLA Ops:
  7.2 27.8 %copy-start = (f32[1024,256]{1,0:T(8,128)S(1)}, f32[1024,256]{1,0:T(8,128)}, u32[]{:S(2)}) copy-start(f32[1024,256]{1,0:T(8,128)} %param.7) | copy-start | bytes 3145732
  7.2 137.8 %all-reduce.3.cloned.1.call-start = ((), (), s32[]{:S(2)}) async-start(), calls=%async_computation | async-start | bytes 2097152 | tf_op jit(solution)/shard_map/psum | solution.py:69
  8.0 4.7 %collective-permute-start.4 = (bf16[1,32,256]{2,1,0:T(8,128)(2,1)S(1)}, bf16[1,32,256]{2,1,0:T(8,128)(2,1)S(1)}, u32[]{:S(2)}, u32[]{:S(2)}) collective-permute-start(bf16[1,32,256]{2,1,0:T(8,128)(2,1)S(1)} %slice.35), channel_id=1, source_target_pairs={{0,1},{1,0},{2,3},{3,2},{4,5},{5,4},{6,7},{7,6},{8,9},{9,8},{10,11... | collective-permute-start | bytes 49160 | tf_op jit(solution)/shard_map/ppermute | solution.py:20
  13.4 3.7 %collective-permute-start = (bf16[1,32,256]{2,1,0:T(8,128)(2,1)S(1)}, bf16[1,32,256]{2,1,0:T(8,128)(2,1)S(1)}, u32[]{:S(2)}, u32[]{:S(2)}) collective-permute-start(bf16[1,32,256]{2,1,0:T(8,128)(2,1)S(1)} %get-tuple-element.112), channel_id=1, source_target_pairs={{0,1},{1,0},{2,3},{3,2},{4,5},{5,4},{6,7},{7,6},{8,9},{9,8},{10,11... | collective-permute-start | bytes 49160 | tf_op jit(solution)/shard_map/ppermute | solution.py:20
  17.9 4.0 %collective-permute-start.1 = (bf16[2,32,256]{2,1,0:T(8,128)(2,1)S(1)}, bf16[2,32,256]{2,1,0:T(8,128)(2,1)S(1)}, u32[]{:S(2)}, u32[]{:S(2)}) collective-permute-start(bf16[2,32,256]{2,1,0:T(8,128)(2,1)S(1)} %pad_maximum_fusion.6), channel_id=1, source_target_pairs={{0,2},{1,3},{2,0},{3,1},{4,6},{5,7},{6,4},{7,5},{8,10},{9,11},{10,... | collective-permute-start | bytes 98312 | tf_op jit(solution)/shard_map/ppermute | solution.py:20
  22.0 5.5 %collective-permute-start.2 = (bf16[4,32,256]{2,1,0:T(8,128)(2,1)S(1)}, bf16[4,32,256]{2,1,0:T(8,128)(2,1)S(1)}, u32[]{:S(2)}, u32[]{:S(2)}) collective-permute-start(bf16[4,32,256]{2,1,0:T(8,128)(2,1)S(1)} %pad_maximum_fusion.4), channel_id=1, source_target_pairs={{0,4},{1,5},{2,6},{3,7},{4,0},{5,1},{6,2},{7,3},{8,12},{9,13},{10,... | collective-permute-start | bytes 196616 | tf_op jit(solution)/shard_map/ppermute | solution.py:20
  24.1 6.1 %collective-permute-start.5 = (bf16[2,32,256]{2,1,0:T(8,128)(2,1)S(1)}, bf16[2,32,256]{2,1,0:T(8,128)(2,1)S(1)}, u32[]{:S(2)}, u32[]{:S(2)}) collective-permute-start(bf16[2,32,256]{2,1,0:T(8,128)(2,1)S(1)} %pad_maximum_fusion.7), channel_id=1, source_target_pairs={{0,2},{1,3},{2,0},{3,1},{4,6},{5,7},{6,4},{7,5},{8,10},{9,11},{10,... | collective-permute-start | bytes 98312 | tf_op jit(solution)/shard_map/ppermute | solution.py:20
  27.5 7.3 %collective-permute-start.3 = (bf16[8,32,256]{2,1,0:T(8,128)(2,1)S(1)}, bf16[8,32,256]{2,1,0:T(8,128)(2,1)S(1)}, u32[]{:S(2)}, u32[]{:S(2)}) collective-permute-start(bf16[8,32,256]{2,1,0:T(8,128)(2,1)S(1)} %pad_maximum_fusion.2), channel_id=1, source_target_pairs={{0,8},{1,9},{2,10},{3,11},{4,12},{5,13},{6,14},{7,15},{8,0},{9,1},... | collective-permute-start | bytes 393224 | tf_op jit(solution)/shard_map/ppermute | solution.py:20
  30.2 97.5 %collective-permute-start.6 = (bf16[4,32,256]{2,1,0:T(8,128)(2,1)S(1)}, bf16[4,32,256]{2,1,0:T(8,128)(2,1)}, u32[]{:S(2)}, u32[]{:S(2)}) collective-permute-start(bf16[4,32,256]{2,1,0:T(8,128)(2,1)S(1)} %pad_maximum_fusion.5), channel_id=1, source_target_pairs={{0,4},{1,5},{2,6},{3,7},{4,0},{5,1},{6,2},{7,3},{8,12},{9,13},{10,... | collective-permute-start | bytes 196616 | tf_op jit(solution)/shard_map/ppermute | solution.py:20
  127.7 116.9 %all-reduce.5.cloned.1.call-start = ((), (), s32[]{:S(2)}) async-start(), calls=%async_computation.1 | async-start | bytes 2097152 | tf_op jit(solution)/shard_map/psum | solution.py:69
  128.7 5.9 %collective-permute-start.7 = (bf16[8,32,256]{2,1,0:T(8,128)(2,1)S(1)}, bf16[8,32,256]{2,1,0:T(8,128)(2,1)S(1)}, u32[]{:S(2)}, u32[]{:S(2)}) collective-permute-start(bf16[8,32,256]{2,1,0:T(8,128)(2,1)S(1)} %pad_maximum_fusion.3), channel_id=1, source_target_pairs={{0,8},{1,9},{2,10},{3,11},{4,12},{5,13},{6,14},{7,15},{8,0},{9,1},... | collective-permute-start | bytes 393224 | tf_op jit(solution)/shard_map/ppermute | solution.py:20
  146.6 1.1 copy-start.1
  225.7 18.9 %copy-start.2 = (f32[1024,256]{1,0:T(8,128)S(1)}, f32[1024,256]{1,0:T(8,128)}, u32[]{:S(2)}) copy-start(f32[1024,256]{1,0:T(8,128)} %copy-done.1) | copy-start | bytes 3145732
Sparse Core Ops, SparseCore 0:
  127.8 17.1 all-reduce.2
  227.4 17.1 all-reduce.4
